TPU v7x, 32 devices: a whole 2x2x4 slice. The times are simulated.
32 devices in a mesh: fsdp: 16 (over z, y, core), dp: 2 (over x).
Axes of the slice: x: 2, y: 2, z: 4, core: 2. Of those that a mesh axis runs over, the one named last changes fastest.
Arguments:
- tokens: bfloat16 [32768, 1024], P(('fsdp', 'dp')), may hold values from -6 to 6
- item_start: int32 [32768], P(('fsdp', 'dp')), may hold values from 0 to 896, as said below
- out_grad: bfloat16 [32768, 1024], P(('fsdp', 'dp')), may hold values from -6 to 6
- norm_gains: float32 [2, 1024], replicated, may hold values from 0.5 to 1.5
- norm_shifts: float32 [2, 1024], replicated, may hold values from -1.25 to 1.25
- w_qkv: bfloat16 [1024, 3072], P('fsdp'), may hold values from -0.1875 to 0.1875
- bias_qkv: float32 [3072], replicated, may hold values from -1.25 to 1.25
- w_out: bfloat16 [1024, 1024], P('fsdp'), may hold values from -0.5 to 0.5
- w_fc: bfloat16 [1024, 4096], P('fsdp'), may hold values from -0.1875 to 0.1875
- bias_fc: float32 [4096], replicated, may hold values from -1.75 to 1.75
- w_proj: bfloat16 [4096, 1024], P('fsdp'), may hold values from -0.09375 to 0.09375
- out_biases: float32 [2, 1024], replicated, may hold values from -1.25 to 1.25
- adapters: float32 [4, 1024, 4], replicated, may hold values from -0.3125 to 0.3125
- momentum: float32 [4, 1024, 4], replicated, may hold values from -1280 to 1280
- average: float32 [4, 1024, 4], replicated, may hold values from -0.3125 to 0.3125
Outputs:
- block_out: bfloat16 [32768, 1024], P(('fsdp', 'dp'))
- in_grad: float32 [32768, 1024], P(('fsdp', 'dp'))
- adapter_grad: float32 [4, 1024, 4], replicated
- new_momentum: float32 [4, 1024, 4], replicated
- new_adapters: float32 [4, 1024, 4], replicated
- new_average: float32 [4, 1024, 4], replicated
- adapter_copy: bfloat16 [4, 1024, 4], replicated
Inputs may be any that keep to these rules, and one draw needn't show every extreme that they name: `item_start`: each device's 1024 rows are cut into aligned runs of 1024 rows, and each run into items of 1024, 512, 256 or 128 rows at aligned places; every row holds the first row of its item, counted within its device. Every draw has an item of 1024 rows and one of 128 rows.
All inputs are finite; a program needn't handle non-finite values.
Results may differ from a plain program's by a relative error of at most 0.014.
The roundings to bfloat16 on the way count: a program that leaves them out, or rounds other values in their place, can miss the bound.
Values may be sent and summed in bfloat16 or wider, within the bound.
A program may use at most 256 MiB of HBM per device.

v0:
```python
import jax
import jax.numpy as jnp
from jax import lax
from jax.sharding import PartitionSpec as P

HEADS = 16
query_span = 512
adapter_scale = 8.0
score_scale = 0.125


def contract_trailing(left, right):
    return lax.dot_general(
        left, right, (((1,), (1,)), ((), ())), preferred_element_type=jnp.float32
    )


def contract_leading(left, right):
    return lax.dot_general(
        left, right, (((0,), (0,)), ((), ())), preferred_element_type=jnp.float32
    )


def layer_norm(values, gain, shift):
    center = values - jnp.mean(values, axis=-1, keepdims=True)
    spread = jnp.mean(center * center, axis=-1, keepdims=True)
    return center * lax.rsqrt(spread + 1e-05) * gain + shift


def gelu_tanh(values):
    return (
        0.5
        * values
        * (1.0 + jnp.tanh(0.7978845608 * (values + 0.044715 * values * values * values)))
    )


def block_scores(query_heads, key_heads, starts, block_index, span_rows):
    row_count = key_heads.shape[0]
    begin_row = block_index * span_rows
    query_block = lax.dynamic_slice_in_dim(query_heads, begin_row, span_rows, 0)
    start_block = lax.dynamic_slice_in_dim(starts, begin_row, span_rows, 0)
    columns = jnp.arange(row_count, dtype=jnp.int32)
    row_ids = begin_row + jnp.arange(span_rows, dtype=jnp.int32)
    scores = (
        jnp.einsum("qhe,khe->hqk", query_block, key_heads, preferred_element_type=jnp.float32)
        * score_scale
    )
    visible = (start_block[:, None] <= columns[None, :]) & (columns[None, :] <= row_ids[:, None])
    return (query_block, jnp.where(visible[None], scores, jnp.float32(-1e30)))


def attend_forward(query_heads, key_heads, value_heads, starts):
    row_count = query_heads.shape[0]
    span_rows = min(query_span, row_count)

    def one_block(block_index):
        query_block, scores = block_scores(query_heads, key_heads, starts, block_index, span_rows)
        highest = jnp.max(scores, axis=-1, keepdims=True)
        raised = jnp.exp(scores - highest)
        totals = jnp.sum(raised, axis=-1, keepdims=True)
        probs = raised / totals
        result = jnp.einsum(
            "hqk,khe->qhe",
            probs.astype(jnp.bfloat16),
            value_heads,
            preferred_element_type=jnp.float32,
        )
        return (result.astype(jnp.bfloat16), (highest + jnp.log(totals))[..., 0])

    outputs, log_sums = lax.map(one_block, jnp.arange(row_count // span_rows, dtype=jnp.int32))
    return (outputs.reshape(query_heads.shape), log_sums)


def attend_backward(query_heads, key_heads, value_heads, grad_heads, log_sums, starts):
    row_count = query_heads.shape[0]
    span_rows = min(query_span, row_count)

    def one_block(carry, block_index):
        grad_keys, value_gradient = carry
        query_block, scores = block_scores(query_heads, key_heads, starts, block_index, span_rows)
        grad_block = lax.dynamic_slice_in_dim(grad_heads, block_index * span_rows, span_rows, 0)
        probs = jnp.exp(scores - log_sums[block_index][:, :, None])
        grad_probs = jnp.einsum(
            "qhe,khe->hqk", grad_block, value_heads, preferred_element_type=jnp.float32
        )
        value_gradient = value_gradient + jnp.einsum(
            "hqk,qhe->khe",
            probs.astype(jnp.bfloat16),
            grad_block,
            preferred_element_type=jnp.float32,
        )
        inner = jnp.sum(probs * grad_probs, axis=-1, keepdims=True)
        grad_scores = (probs * (grad_probs - inner)).astype(jnp.bfloat16)
        query_gradient = (
            jnp.einsum("hqk,khe->qhe", grad_scores, key_heads, preferred_element_type=jnp.float32)
            * score_scale
        )
        grad_keys = (
            grad_keys
            + jnp.einsum(
                "hqk,qhe->khe", grad_scores, query_block, preferred_element_type=jnp.float32
            )
            * score_scale
        )
        return ((grad_keys, value_gradient), query_gradient.astype(jnp.bfloat16))

    zeros_heads = jnp.zeros(key_heads.shape, jnp.float32)
    (grad_keys, value_gradient), grad_queries = lax.scan(
        one_block, (zeros_heads, zeros_heads), jnp.arange(row_count // span_rows, dtype=jnp.int32)
    )
    return (
        grad_queries.reshape(query_heads.shape),
        grad_keys.astype(jnp.bfloat16),
        value_gradient.astype(jnp.bfloat16),
    )


def per_device(
    tokens,
    item_start,
    out_grad,
    norm_gains,
    norm_shifts,
    w_qkv,
    bias_qkv,
    w_out,
    w_fc,
    bias_fc,
    w_proj,
    out_biases,
    adapters,
    momentum,
    average,
):
    row_count, hidden_width = tokens.shape
    head_size = hidden_width // HEADS
    qkv_full, out_full = (
        lax.all_gather(w_qkv, "fsdp", axis=0, tiled=True),
        lax.all_gather(w_out, "fsdp", axis=0, tiled=True),
    )
    fc_full, proj_full = (
        lax.all_gather(w_fc, "fsdp", axis=0, tiled=True),
        lax.all_gather(w_proj, "fsdp", axis=0, tiled=True),
    )
    reduced_adapter_pass = adapters.astype(jnp.bfloat16)
    residual = tokens.astype(jnp.float32)

    def norm_first(values):
        return layer_norm(values, norm_gains[0], norm_shifts[0])

    def norm_second(values):
        return layer_norm(values, norm_gains[1], norm_shifts[1])

    normed_one, back_first = jax.vjp(norm_first, residual)
    normed_one = normed_one.astype(jnp.bfloat16)
    mixed_tokens_full = jnp.dot(normed_one, qkv_full, preferred_element_type=jnp.float32) + bias_qkv
    query_down_matrix = jnp.dot(
        normed_one, reduced_adapter_pass[0], preferred_element_type=jnp.float32
    ).astype(jnp.bfloat16)
    value_down_matrix = jnp.dot(
        normed_one, reduced_adapter_pass[2], preferred_element_type=jnp.float32
    ).astype(jnp.bfloat16)
    query_rows = (
        mixed_tokens_full[:, :hidden_width]
        + adapter_scale * contract_trailing(query_down_matrix, reduced_adapter_pass[1])
    ).astype(jnp.bfloat16)
    keys_all = mixed_tokens_full[:, hidden_width : 2 * hidden_width].astype(jnp.bfloat16)
    value_rows_full = (
        mixed_tokens_full[:, 2 * hidden_width :]
        + adapter_scale * contract_trailing(value_down_matrix, reduced_adapter_pass[3])
    ).astype(jnp.bfloat16)
    heads_shape = (row_count, HEADS, head_size)
    query_heads = query_rows.reshape(heads_shape)
    key_heads = keys_all.reshape(heads_shape)
    value_heads = value_rows_full.reshape(heads_shape)
    attended, log_sums = attend_forward(query_heads, key_heads, value_heads, item_start)
    attended = attended.reshape(row_count, hidden_width)
    middle = (
        residual + jnp.dot(attended, out_full, preferred_element_type=jnp.float32) + out_biases[0]
    )
    normed_two, back_second = jax.vjp(norm_second, middle)
    normed_two = normed_two.astype(jnp.bfloat16)
    pre_act = jnp.dot(normed_two, fc_full, preferred_element_type=jnp.float32) + bias_fc
    activation, back_gelu = jax.vjp(gelu_tanh, pre_act)
    activation = activation.astype(jnp.bfloat16)
    result = (
        middle + jnp.dot(activation, proj_full, preferred_element_type=jnp.float32) + out_biases[1]
    )
    block_out = result.astype(jnp.bfloat16)
    fc_back, proj_back = (
        lax.all_gather(w_fc, "fsdp", axis=0, tiled=True),
        lax.all_gather(w_proj, "fsdp", axis=0, tiled=True),
    )
    qkv_back, out_back = (
        lax.all_gather(w_qkv, "fsdp", axis=0, tiled=True),
        lax.all_gather(w_out, "fsdp", axis=0, tiled=True),
    )
    grad_act = contract_trailing(out_grad, proj_back)
    grad_pre = back_gelu(grad_act)[0].astype(jnp.bfloat16)
    grad_norm_two = contract_trailing(grad_pre, fc_back)
    grad_middle = out_grad.astype(jnp.float32) + back_second(grad_norm_two)[0]
    grad_branch = grad_middle.astype(jnp.bfloat16)
    grad_attended = (
        contract_trailing(grad_branch, out_back).astype(jnp.bfloat16).reshape(heads_shape)
    )
    query_gradient, grad_keys, value_gradient = attend_backward(
        query_heads, key_heads, value_heads, grad_attended, log_sums, item_start
    )
    query_gradient = query_gradient.reshape(row_count, hidden_width)
    grad_keys = grad_keys.reshape(row_count, hidden_width)
    value_gradient = value_gradient.reshape(row_count, hidden_width)
    grad_mixed = jnp.concatenate([query_gradient, grad_keys, value_gradient], axis=1)
    grad_down_q = (
        adapter_scale
        * jnp.dot(query_gradient, reduced_adapter_pass[1], preferred_element_type=jnp.float32)
    ).astype(jnp.bfloat16)
    grad_down_v = (
        adapter_scale
        * jnp.dot(value_gradient, reduced_adapter_pass[3], preferred_element_type=jnp.float32)
    ).astype(jnp.bfloat16)
    grad_norm_one = (
        contract_trailing(grad_mixed, qkv_back)
        + contract_trailing(grad_down_q, reduced_adapter_pass[0])
        + contract_trailing(grad_down_v, reduced_adapter_pass[2])
    )
    in_grad = grad_middle + back_first(grad_norm_one)[0]
    local_grads = jnp.stack(
        [
            contract_leading(normed_one, grad_down_q),
            adapter_scale * contract_leading(query_gradient, query_down_matrix),
            contract_leading(normed_one, grad_down_v),
            adapter_scale * contract_leading(value_gradient, value_down_matrix),
        ]
    )
    adapter_grad = lax.psum(local_grads, ("fsdp", "dp"))
    tokens_total = row_count * lax.axis_size("fsdp") * lax.axis_size("dp")
    step_rate = 0.01 / jnp.sqrt(jnp.float32(tokens_total))
    new_momentum = 0.9 * momentum + adapter_grad
    new_adapters = adapters - step_rate * (adapter_grad + 0.9 * new_momentum)
    new_average = 0.9 * average + 0.1 * new_adapters
    return (
        block_out,
        in_grad,
        adapter_grad,
        new_momentum,
        new_adapters,
        new_average,
        new_adapters.astype(jnp.bfloat16),
    )


def solution(mesh):
    in_specs = (
        P(("fsdp", "dp"), None),
        P(("fsdp", "dp")),
        P(("fsdp", "dp"), None),
        P(),
        P(),
        P("fsdp", None),
        P(),
        P("fsdp", None),
        P("fsdp", None),
        P(),
        P("fsdp", None),
        P(),
        P(),
        P(),
        P(),
    )
    out_specs = (P(("fsdp", "dp"), None), P(("fsdp", "dp"), None), P(), P(), P(), P(), P())
    return jax.shard_map(
        per_device, mesh=mesh, in_specs=in_specs, out_specs=out_specs, check_vma=False
    )
```

profile of v0, /device:TPU:1, one launch (start us, length us, event | category | flops | bytes accessed | tf_op | source)
XLA Modules:
  0.0 687.8 jit_solution(17003402721910862022)
XLA Ops:
  23.1 51.6 %all-gather.5.cloned.1.call-done = bf16[1024,3072]{1,0:T(8,128)(2,1)} async-done(((bf16[64,3072]{1,0:T(8,128)(2,1)}), bf16[1024,3072]{1,0:T(8,128)(2,1)}) %all-gather.5.cloned.1.call-update) | async-done | bytes 6291472 | tf_op jit(solution)/shard_map/all_gather | solution.py:139
  74.7 9.0 %broadcast_add_fusion = f32[1024,3072]{1,0:T(8,128)S(1)} fusion(f32[3072]{0:T(1024)S(1)} %copy-done.48, bf16[1024,1024]{0,1:T(8,128)(2,1)S(1)} %copy-done.5, bf16[1024,3072]{1,0:T(8,128)(2,1)} %all-gather.5.cloned.1.call-done), kind=kOutput, calls=%fused_computation.68 | convolution fusion | flops 6445596672 | bytes 20983808 | tf_op jit(solution)/shard_map/dot_general | solution.py:157
  104.8 100.2 %while.27 = (s32[]{:T(128)}, bf16[2,512,16,64]{1,3,2,0:T(8,128)(2,1)}, f32[2,16,512]{2,1,0:T(8,128)S(1)}, s32[2]{0:T(128)S(1)}, s32[1024]{0:T(1024)}, /*index=5*...) while((s32[]{:T(128)}, ...), condition=%wide.region_5.6_spmd, body=%wide.region_2.5_spmd.sunk | while | flops 2250236416 | bytes 134490384 | solution.py:71
  107.6 15.3 %fusion.152 = (f32[16,512]{1,0:T(8,128)S(1)}, f32[16,512,1024]{2,1,0:T(8,128)}) fusion(pred[512,1024]{1,0:T(8,128)(4,1)S(1)} %fusion.151, bf16[1024,16,64]{0,2,1:T(8,128)(2,1)S(1)} %get-tuple-element.396, bf16[1024,16,64]{0,2,1:T(8,128)(2,1)} %get-tuple-element.395, s32[]{:T(128)S(6)} %select_n.60), kind=kOutput, calls=%fused_computation.3.clone.1 | convolution fusion | flops 1098899456 | bytes 37257220 | tf_op jit(solution)/shard_map/while/body/eval_jaxpr/qhe,khe->hqk/dot_general | solution.py:46
  122.9 15.9 %fusion.153 = f32[16,512]{1,0:T(8,128)S(1)} fusion(f32[16,512,1024]{2,1,0:T(8,128)} %get-tuple-element.351, f32[16,512]{1,0:T(8,128)S(1)} %get-tuple-element.352, pred[512,1024]{1,0:T(8,128)(4,1)S(1)} %fusion.151), kind=kLoop, calls=%fused_computation.4.clone.1 | loop fusion | flops 33546240 | bytes 34144256 | tf_op jit(solution)/shard_map/while/body/eval_jaxpr/reduce_sum | solution.py:61
  138.8 14.7 %fusion.154 = bf16[2,512,16,64]{1,3,2,0:T(8,128)(2,1)S(1)} fusion(bf16[2,512,16,64]{1,3,2,0:T(8,128)(2,1)S(1)} %copy-done.12, s32[]{:T(128)S(6)} %copy.58, bf16[1024,16,64]{0,2,1:T(8,128)(2,1)S(1)} %copy-done.1, f32[16,512,1024]{2,1,0:T(8,128)} %get-tuple-element.351, f32[16,512]{1,0:T(8,128)S(1)} %fusion.153, ...), kind=kOutput, calls=%fused_computation.11.clone.1 | convolution fusion | flops 1116209152 | bytes 37289988 | tf_op jit(solution)/shard_map/while/body/eval_jaxpr/hqk,khe->qhe/dot_general | solution.py:63
  157.4 15.5 %fusion.152 = (f32[16,512]{1,0:T(8,128)S(1)}, f32[16,512,1024]{2,1,0:T(8,128)}) fusion(pred[512,1024]{1,0:T(8,128)(4,1)S(1)} %fusion.151, bf16[1024,16,64]{0,2,1:T(8,128)(2,1)S(1)} %get-tuple-element.396, bf16[1024,16,64]{0,2,1:T(8,128)(2,1)} %get-tuple-element.395, s32[]{:T(128)S(6)} %select_n.60), kind=kOutput, calls=%fused_computation.3.clone.1 | convolution fusion | flops 1098899456 | bytes 37257220 | tf_op jit(solution)/shard_map/while/body/eval_jaxpr/qhe,khe->hqk/dot_general | solution.py:46
  172.9 15.7 %fusion.153 = f32[16,512]{1,0:T(8,128)S(1)} fusion(f32[16,512,1024]{2,1,0:T(8,128)} %get-tuple-element.351, f32[16,512]{1,0:T(8,128)S(1)} %get-tuple-element.352, pred[512,1024]{1,0:T(8,128)(4,1)S(1)} %fusion.151), kind=kLoop, calls=%fused_computation.4.clone.1 | loop fusion | flops 33546240 | bytes 34144256 | tf_op jit(solution)/shard_map/while/body/eval_jaxpr/reduce_sum | solution.py:61
  188.6 14.8 %fusion.154 = bf16[2,512,16,64]{1,3,2,0:T(8,128)(2,1)S(1)} fusion(bf16[2,512,16,64]{1,3,2,0:T(8,128)(2,1)S(1)} %copy-done.12, s32[]{:T(128)S(6)} %copy.58, bf16[1024,16,64]{0,2,1:T(8,128)(2,1)S(1)} %copy-done.1, f32[16,512,1024]{2,1,0:T(8,128)} %get-tuple-element.351, f32[16,512]{1,0:T(8,128)S(1)} %fusion.153, ...), kind=kOutput, calls=%fused_computation.11.clone.1 | convolution fusion | flops 1116209152 | bytes 37289988 | tf_op jit(solution)/shard_map/while/body/eval_jaxpr/hqk,khe->qhe/dot_general | solution.py:63
  210.6 5.7 fusion.94
  218.9 16.9 %fusion.63 = f32[1024,4096]{1,0:T(8,128)} fusion(bf16[1024,4096]{1,0:T(8,128)(2,1)} %all-gather.9.cloned.1.call-done, f32[1024,1024]{0,1:T(8,128)} %copy-done.8, f32[1024]{0:T(1024)S(1)} %bitcast.155, f32[1024]{0:T(1024)S(1)} %bitcast.150, f32[1024]{0:T(1024)S(1)} %fusion.79, f32[1024]{0:T(1024)S(1)} %broadcast_multiply_fusion), kind=kOutput, calls=%fused_computation.96 | convolution fusion | flops 8595177472 | bytes 29376512 | tf_op jit(solution)/shard_map/dot_general | solution.py:184
  235.8 32.2 %all-gather.11.cloned.1.call-done = bf16[4096,1024]{1,0:T(8,128)(2,1)} async-done(((bf16[256,1024]{1,0:T(8,128)(2,1)}), bf16[4096,1024]{1,0:T(8,128)(2,1)}) %all-gather.11.cloned.1.call-update) | async-done | bytes 8388624 | tf_op jit(solution)/shard_map/all_gather | solution.py:144
  268.0 33.9 %multiply_reduce_fusion.1 = (f32[1024]{0:T(1024)S(1)}, f32[1024,1024]{0,1:T(8,128)}) fusion(f32[1024,1024]{0,1:T(8,128)} %copy-done.8, f32[1024]{0:T(1024)S(1)} %bitcast.151, f32[1024]{0:T(1024)S(1)} %broadcast_multiply_fusion, bf16[1024,4096]{1,0:T(8,128)(2,1)} %all-gather.9.cloned.1.call-done, f32[1024,4096]{1,0:T(8,128)} %fusion.63, ...), kind=kOutput, calls=%fused_computation.90 | convolution fusion | flops 17288921088 | bytes 44068864 | tf_op jit(solution)/shard_map/dot_general | solution.py:13
  301.9 4.7 fusion.90
  311.9 224.5 %while.28 = (s32[]{:T(128)}, f32[1024,16,64]{0,2,1:T(8,128)}, f32[1024,16,64]{0,2,1:T(8,128)}, bf16[2,512,16,64]{1,3,2,0:T(8,128)(2,1)}, s32[2]{0:T(128)S(1)}, /...) while((s32[]{:T(128)}, f32[1024,16,64]{0,2,1:T(8,128)}, ...), condition=%wide.region_12.13_spmd.clone, body=%wide.region_10.12_spmd.clone.sunk | while | flops 5502394880 | bytes 282831200 | solution.py:109
  313.3 14.4 %fusion.164 = f32[16,512,1024]{2,1,0:T(8,128)} fusion(bf16[1024,16,64]{0,2,1:T(8,128)(2,1)S(1)} %get-tuple-element.441, bf16[1024,16,64]{0,2,1:T(8,128)(2,1)} %get-tuple-element.439, s32[]{:T(128)S(6)} %select_n.64), kind=kOutput, calls=%fused_computation.37.clone.1 | convolution fusion | flops 1073741824 | bytes 36700164 | tf_op jit(solution)/shard_map/while/body/eval_jaxpr/qhe,khe->hqk/dot_general | solution.py:46
  330.8 26.0 %multiply_reduce_fusion.4 = (f32[16,512]{1,0:T(8,128)S(1)}, f32[16,512,1024]{2,1,0:T(8,128)}) fusion(f32[16,512,1024]{2,1,0:T(8,128)} %fusion.164, f32[16,512]{1,0:T(8,128)S(1)} %dynamic-slice_bitcast_fusion.2, pred[512,1024]{1,0:T(8,128)(4,1)S(1)} %fusion.165, bf16[1024,16,64]{0,2,1:T(8,128)(2,1)} %get-tuple-element.444, ...), kind=kOutput, calls=%fused_computation.20.clone.1 | convolution fusion | flops 1115676672 | bytes 70844416 | tf_op jit(solution)/shard_map/while/body/eval_jaxpr/qhe,khe->hqk/dot_general | solution.py:84
  356.8 27.8 %multiply_convert_fusion.7 = bf16[16,512,1024]{2,1,0:T(8,128)(2,1)} fusion(f32[16,512,1024]{2,1,0:T(8,128)} %get-tuple-element.364, f32[16,512,1024]{2,1,0:T(8,128)} %fusion.164, f32[16,512]{1,0:T(8,128)S(1)} %get-tuple-element.365, f32[16,512]{1,0:T(8,128)S(1)} %dynamic-slice_bitcast_fusion.2, pred[512,1024]{1,0:T(8,128)(4,1)S(1)} %fusion.165), kind=kLoop, calls=%fused_computation.19.clone.1 | loop fusion | flops 50331648 | bytes 84475904 | tf_op jit(solution)/shard_map/while/body/eval_jaxpr/convert_element_type | solution.py:94
  384.6 11.1 %bitcast_add_fusion.4 = f32[1024,16,64]{0,2,1:T(8,128)} fusion(f32[1024,16,64]{0,2,1:T(8,128)} %get-tuple-element.419, bf16[16,512,1024]{2,1,0:T(8,128)(2,1)} %multiply_convert_fusion.7, pred[]{:T(512)S(6)} %compare.3, bf16[1024,16,64]{0,2,1:T(8,128)(2,1)} %get-tuple-element.439, s32[]{:T(128)S(6)} %select_n.64), kind=kOutput, calls=%fused_computation.26.clone.1 | convolution fusion | flops 1076887552 | bytes 26214404 | tf_op jit(solution)/shard_map/while/body/eval_jaxpr/hqk,qhe->khe/dot_general | solution.py:101
  395.7 17.5 %bitcast_add_fusion.5 = f32[1024,16,64]{0,2,1:T(8,128)} fusion(f32[1024,16,64]{0,2,1:T(8,128)} %get-tuple-element.420, f32[16,512,1024]{2,1,0:T(8,128)} %fusion.164, f32[16,512]{1,0:T(8,128)S(1)} %dynamic-slice_bitcast_fusion.2, pred[512,1024]{1,0:T(8,128)(4,1)S(1)} %fusion.165, pred[]{:T(512)S(6)} %compare.3, ...), kind=kOutput, calls=%fused_computation.25.clone.1 | convolution fusion | flops 1109393408 | bytes 43548676 | tf_op jit(solution)/shard_map/while/body/eval_jaxpr/hqk,qhe->khe/dot_general | solution.py:87
  413.2 9.8 %fusion.166 = bf16[2,512,16,64]{1,3,2,0:T(8,128)(2,1)} fusion(bf16[2,512,16,64]{1,3,2,0:T(8,128)(2,1)} %get-tuple-element.421, s32[]{:T(128)S(6)} %copy.68, bf16[16,512,1024]{2,1,0:T(8,128)(2,1)} %multiply_convert_fusion.7, bf16[1024,16,64]{0,2,1:T(8,128)(2,1)S(1)} %get-tuple-element.441), kind=kOutput, calls=%fused_computation.32.clone.1 | convolution fusion | flops 1074790400 | bytes 19922948 | tf_op jit(solution)/shard_map/while/body/eval_jaxpr/hqk,khe->qhe/dot_general | solution.py:96
  424.1 14.4 %fusion.164 = f32[16,512,1024]{2,1,0:T(8,128)} fusion(bf16[1024,16,64]{0,2,1:T(8,128)(2,1)S(1)} %get-tuple-element.441, bf16[1024,16,64]{0,2,1:T(8,128)(2,1)} %get-tuple-element.439, s32[]{:T(128)S(6)} %select_n.64), kind=kOutput, calls=%fused_computation.37.clone.1 | convolution fusion | flops 1073741824 | bytes 36700164 | tf_op jit(solution)/shard_map/while/body/eval_jaxpr/qhe,khe->hqk/dot_general | solution.py:46
  441.7 26.0 %multiply_reduce_fusion.4 = (f32[16,512]{1,0:T(8,128)S(1)}, f32[16,512,1024]{2,1,0:T(8,128)}) fusion(f32[16,512,1024]{2,1,0:T(8,128)} %fusion.164, f32[16,512]{1,0:T(8,128)S(1)} %dynamic-slice_bitcast_fusion.2, pred[512,1024]{1,0:T(8,128)(4,1)S(1)} %fusion.165, bf16[1024,16,64]{0,2,1:T(8,128)(2,1)} %get-tuple-element.444, ...), kind=kOutput, calls=%fused_computation.20.clone.1 | convolution fusion | flops 1115676672 | bytes 70844416 | tf_op jit(solution)/shard_map/while/body/eval_jaxpr/qhe,khe->hqk/dot_general | solution.py:84
  467.6 27.8 %multiply_convert_fusion.7 = bf16[16,512,1024]{2,1,0:T(8,128)(2,1)} fusion(f32[16,512,1024]{2,1,0:T(8,128)} %get-tuple-element.364, f32[16,512,1024]{2,1,0:T(8,128)} %fusion.164, f32[16,512]{1,0:T(8,128)S(1)} %get-tuple-element.365, f32[16,512]{1,0:T(8,128)S(1)} %dynamic-slice_bitcast_fusion.2, pred[512,1024]{1,0:T(8,128)(4,1)S(1)} %fusion.165), kind=kLoop, calls=%fused_computation.19.clone.1 | loop fusion | flops 50331648 | bytes 84475904 | tf_op jit(solution)/shard_map/while/body/eval_jaxpr/convert_element_type | solution.py:94
  495.4 12.3 %bitcast_add_fusion.4 = f32[1024,16,64]{0,2,1:T(8,128)} fusion(f32[1024,16,64]{0,2,1:T(8,128)} %get-tuple-element.419, bf16[16,512,1024]{2,1,0:T(8,128)(2,1)} %multiply_convert_fusion.7, pred[]{:T(512)S(6)} %compare.3, bf16[1024,16,64]{0,2,1:T(8,128)(2,1)} %get-tuple-element.439, s32[]{:T(128)S(6)} %select_n.64), kind=kOutput, calls=%fused_computation.26.clone.1 | convolution fusion | flops 1076887552 | bytes 26214404 | tf_op jit(solution)/shard_map/while/body/eval_jaxpr/hqk,qhe->khe/dot_general | solution.py:101
  507.8 18.7 %bitcast_add_fusion.5 = f32[1024,16,64]{0,2,1:T(8,128)} fusion(f32[1024,16,64]{0,2,1:T(8,128)} %get-tuple-element.420, f32[16,512,1024]{2,1,0:T(8,128)} %fusion.164, f32[16,512]{1,0:T(8,128)S(1)} %dynamic-slice_bitcast_fusion.2, pred[512,1024]{1,0:T(8,128)(4,1)S(1)} %fusion.165, pred[]{:T(512)S(6)} %compare.3, ...), kind=kOutput, calls=%fused_computation.25.clone.1 | convolution fusion | flops 1109393408 | bytes 43548676 | tf_op jit(solution)/shard_map/while/body/eval_jaxpr/hqk,qhe->khe/dot_general | solution.py:87
  526.5 9.8 %fusion.166 = bf16[2,512,16,64]{1,3,2,0:T(8,128)(2,1)} fusion(bf16[2,512,16,64]{1,3,2,0:T(8,128)(2,1)} %get-tuple-element.421, s32[]{:T(128)S(6)} %copy.68, bf16[16,512,1024]{2,1,0:T(8,128)(2,1)} %multiply_convert_fusion.7, bf16[1024,16,64]{0,2,1:T(8,128)(2,1)S(1)} %get-tuple-element.441), kind=kOutput, calls=%fused_computation.32.clone.1 | convolution fusion | flops 1074790400 | bytes 19922948 | tf_op jit(solution)/shard_map/while/body/eval_jaxpr/hqk,khe->qhe/dot_general | solution.py:96
  547.8 6.7 fusion.42
  559.9 17.0 %add_convert_fusion = bf16[1024,1024]{0,1:T(8,128)(2,1)} fusion(f32[1024,1024]{0,1:T(8,128)} %copy-done.8, f32[1024]{0:T(1024)S(1)} %bitcast.154, bf16[4096,1024]{1,0:T(8,128)(2,1)} %all-gather.11.cloned.1.call-done, f32[1024,4096]{1,0:T(8,128)} %fusion.63, f32[4096]{0:T(1024)S(1)} %copy-done.47), kind=kOutput, calls=%fused_computation.91 | convolution fusion | flops 8635023360 | bytes 31477760 | tf_op jit(solution)/shard_map/dot_general | solution.py:188
  576.9 7.8 %add_add_fusion.2 = f32[1024,1024]{0,1:T(8,128)} fusion(f32[1024,1024]{0,1:T(8,128)} %copy-done.9, bf16[1024,1024]{0,1:T(8,128)(2,1)} %copy.43, f32[1024]{0:T(1024)S(1)} %negate_multiply_fusion, f32[1024]{0:T(1024)S(1)} %copy-done.38, f32[1024]{0:T(1024)S(1)} %multiply_multiply_fusion.2, f32[1024]{0:T(1024)S(1)} %copy-done.23, ...), kind=kLoop, calls=%fused_computation.87 | loop fusion | flops 11534336 | bytes 16797696 | tf_op jit(solution)/shard_map/add | solution.py:227
  588.6 5.4 copy.46
  594.0 83.1 %all-reduce.2.cloned.1.call-done = f32[4,1024,4]{1,2,0:T(4,128)} async-done(((f32[4,1024,4]{1,2,0:T(4,128)}), f32[4,1024,4]{1,2,0:T(4,128)}) %all-reduce.2.cloned.1.call-update) | async-done | bytes 65552 | tf_op jit(solution)/shard_map/psum | solution.py:236
  (199 shorter events, 85.0 us)
Async XLA Ops:
  7.2 5.8 copy-start.39
  7.2 6.4 copy-start.40
  7.2 67.5 %all-gather.5.cloned.1.call-start = ((), (), s32[]{:S(2)}) async-start(), calls=%async_computation | async-start | bytes 6684672 | tf_op jit(solution)/shard_map/all_gather | solution.py:139
  7.9 202.7 %all-gather.7.cloned.1.call-start = ((), (), s32[]{:S(2)}) async-start(), calls=%async_computation.1 | async-start | bytes 2228224 | tf_op jit(solution)/shard_map/all_gather | solution.py:140
  8.7 210.2 %all-gather.9.cloned.1.call-start = ((), (), s32[]{:S(2)}) async-start(), calls=%async_computation.2 | async-start | bytes 8912896 | tf_op jit(solution)/shard_map/all_gather | solution.py:143
  9.4 258.6 %all-gather.11.cloned.1.call-start = ((), (), s32[]{:S(2)}) async-start(), calls=%async_computation.3 | async-start | bytes 8912896 | tf_op jit(solution)/shard_map/all_gather | solution.py:144
  10.0 667.2 %all-reduce.2.cloned.1.call-start = ((), (), s32[]{:S(2)}) async-start(), calls=%async_computation.4 | async-start | bytes 131072 | tf_op jit(solution)/shard_map/psum | solution.py:236
  10.0 5.8 copy-start.20
  15.9 79.2 %copy-start.17 = (bf16[4,1024,4]{1,2,0:T(4,128)(2,1)}, bf16[4,1024,4]{1,2,0:T(4,128)(2,1)S(1)}, u32[]{:S(2)}) copy-start(bf16[4,1024,4]{1,2,0:T(4,128)(2,1)S(1)} %convert_element_type.81) | copy-start | bytes 98308
  16.7 58.0 %copy-start.48 = (f32[3072]{0:T(1024)S(1)}, f32[3072]{0:T(1024)}, u32[]{:S(2)}) copy-start(f32[3072]{0:T(1024)} %param.25) | copy-start | bytes 36868
  18.0 67.5 %copy-start.24 = (bf16[1024,4]{0,1:T(4,128)(2,1)}, bf16[1024,4]{0,1:T(4,128)(2,1)S(1)}, u32[]{:S(2)}) copy-start(bf16[1024,4]{0,1:T(4,128)(2,1)S(1)} %convolution_convert_fusion.1) | copy-start | bytes 24580
  18.4 76.6 %copy-start.26 = (bf16[1024,4]{0,1:T(4,128)(2,1)}, bf16[1024,4]{0,1:T(4,128)(2,1)S(1)}, u32[]{:S(2)}) copy-start(bf16[1024,4]{0,1:T(4,128)(2,1)S(1)} %convolution_convert_fusion) | copy-start | bytes 24580
  18.4 56.3 %copy-start.5 = (bf16[1024,1024]{0,1:T(8,128)(2,1)S(1)}, bf16[1024,1024]{0,1:T(8,128)(2,1)}, u32[]{:S(2)}) copy-start(bf16[1024,1024]{0,1:T(8,128)(2,1)} %copy-done.4) | copy-start | bytes 6291460
  83.7 5.2 copy-start.10
  122.9 15.9 %copy-start.1 = (bf16[1024,16,64]{0,2,1:T(8,128)(2,1)S(1)}, bf16[1024,16,64]{0,2,1:T(8,128)(2,1)}, u32[]{:S(2)}) copy-start(bf16[1024,16,64]{0,2,1:T(8,128)(2,1)} %get-tuple-element.397) | copy-start | bytes 6291460 | tf_op jit(solution)/shard_map/while
  122.9 15.9 %copy-start.12 = (bf16[2,512,16,64]{1,3,2,0:T(8,128)(2,1)S(1)}, bf16[2,512,16,64]{1,3,2,0:T(8,128)(2,1)}, u32[]{:S(2)}) copy-start(bf16[2,512,16,64]{1,3,2,0:T(8,128)(2,1)} %get-tuple-element.379) | copy-start | bytes 6291460 | tf_op jit(solution)/shard_map/while
  172.9 15.7 %copy-start.1 = (bf16[1024,16,64]{0,2,1:T(8,128)(2,1)S(1)}, bf16[1024,16,64]{0,2,1:T(8,128)(2,1)}, u32[]{:S(2)}) copy-start(bf16[1024,16,64]{0,2,1:T(8,128)(2,1)} %get-tuple-element.397) | copy-start | bytes 6291460 | tf_op jit(solution)/shard_map/while
  172.9 15.7 %copy-start.12 = (bf16[2,512,16,64]{1,3,2,0:T(8,128)(2,1)S(1)}, bf16[2,512,16,64]{1,3,2,0:T(8,128)(2,1)}, u32[]{:S(2)}) copy-start(bf16[2,512,16,64]{1,3,2,0:T(8,128)(2,1)} %get-tuple-element.379) | copy-start | bytes 6291460 | tf_op jit(solution)/shard_map/while
  205.0 5.7 copy-start.44
  218.9 49.0 %copy-start.46 = (f32[4096]{0:T(1024)S(1)}, f32[4096]{0:T(1024)}, u32[]{:S(2)}) copy-start(f32[4096]{0:T(1024)} %param.28) | copy-start | bytes 49156
  301.9 4.7 copy-start.45
  312.1 17.3 %copy-start.15 = (f32[2,16,512]{2,1,0:T(8,128)}, f32[2,16,512]{2,1,0:T(8,128)S(1)}, u32[]{:S(2)}) copy-start(f32[2,16,512]{2,1,0:T(8,128)S(1)} %get-tuple-element.442) | copy-start | bytes 196612 | tf_op jit(solution)/shard_map/while
  413.2 9.8 %copy-start.16 = (f32[2,16,512]{2,1,0:T(8,128)S(1)}, f32[2,16,512]{2,1,0:T(8,128)}, u32[]{:S(2)}) copy-start(f32[2,16,512]{2,1,0:T(8,128)} %copy-done.15) | copy-start | bytes 196612 | tf_op jit(solution)/shard_map/while
  423.0 17.3 %copy-start.15 = (f32[2,16,512]{2,1,0:T(8,128)}, f32[2,16,512]{2,1,0:T(8,128)S(1)}, u32[]{:S(2)}) copy-start(f32[2,16,512]{2,1,0:T(8,128)S(1)} %get-tuple-element.442) | copy-start | bytes 196612 | tf_op jit(solution)/shard_map/while
  526.5 9.8 %copy-start.16 = (f32[2,16,512]{2,1,0:T(8,128)S(1)}, f32[2,16,512]{2,1,0:T(8,128)}, u32[]{:S(2)}) copy-start(f32[2,16,512]{2,1,0:T(8,128)} %copy-done.15) | copy-start | bytes 196612 | tf_op jit(solution)/shard_map/while
  547.8 6.7 copy-start.3
  547.8 6.7 copy-start.23
  547.8 6.8 copy-start.35
  559.9 17.0 %copy-start.38 = (f32[1024]{0:T(1024)S(1)}, f32[1024]{0:T(1024)}, u32[]{:S(2)}) copy-start(f32[1024]{0:T(1024)} %copy-done.37) | copy-start | bytes 12292
  588.6 88.5 %copy-start.21 = (f32[4,1024,4]{1,2,0:T(4,128)S(1)}, f32[4,1024,4]{1,2,0:T(4,128)}, u32[]{:S(2)}) copy-start(f32[4,1024,4]{1,2,0:T(4,128)} %param.31) | copy-start | bytes 196612
  588.6 88.5 %copy-start.29 = (f32[4,1024,4]{1,2,0:T(4,128)S(1)}, f32[4,1024,4]{1,2,0:T(4,128)}, u32[]{:S(2)}) copy-start(f32[4,1024,4]{1,2,0:T(4,128)} %param.32) | copy-start | bytes 196612
  588.6 90.1 %copy-start.28 = (f32[4,1024,4]{1,2,0:T(4,128)S(1)}, f32[4,1024,4]{1,2,0:T(4,128)}, u32[]{:S(2)}) copy-start(f32[4,1024,4]{1,2,0:T(4,128)} %param.33) | copy-start | bytes 196612
  (29 other events, 73.2 us)
Sparse Core Ops, SparseCore 0:
  10.3 64.3 all-gather.4
  76.9 39.9 all-gather.6
  119.0 73.7 all-gather.8
  194.8 73.1 all-gather.10
  560.0 117.0 all-reduce.1
where the time goes:
time: 696 us; the launch traced here: 688 us
  matrix products  325 us (47%)
  waiting for transfers between devices  169 us (24%)
  other arithmetic  111 us (16%)
  local copies, waits for them, and re-layouts  60.7 us (9%)
  between operations  14.8 us (2%)
    psum x1, waiting for transfers between devices, per_device(): adapter_grad = lax.psum(local_grads, ('fsdp', 'dp'))  83.1 us
    dot_general x4, matrix products, block_scores(): jnp.einsum('qhe,khe->hqk', query_block, key_heads, preferred_element_type...  59.7 us
    convert_element_type x2, other arithmetic, one_block(): grad_scores = (probs * (grad_probs - inner)).astype(jnp.bfloat16)  55.6 us
    dot_general x2, matrix products, one_block(): jnp.einsum('qhe,khe->hqk', grad_block, value_heads, preferred_element_typ...  52 us
    dot_general x7, matrix products, contract_trailing(): lax.dot_general(left, right, (((1,), (1,)), ((), ())), preferred_element_...  51.8 us
    all_gather x1, waiting for transfers between devices, per_device(): lax.all_gather(w_qkv, 'fsdp', axis=0, tiled=True)  51.6 us
    dot_general x2, matrix products, one_block(): jnp.einsum('hqk,qhe->khe', probs.astype(jnp.bfloat16), grad_block, prefer...  36.3 us
    all_gather x1, waiting for transfers between devices, per_device(): lax.all_gather(w_proj, 'fsdp', axis=0, tiled=True)  32.2 us
  transfers between devices with their start and end apart: 5, of which 3 were waited for; matrix products, arithmetic and copies ran while one was open for 29% of the time, Pallas kernels for 0%

commit v1 on v0

--- a/solution.py
+++ b/solution.py
@@ -233,7 +233,7 @@
             adapter_scale * contract_leading(value_gradient, value_down_matrix),
         ]
     )
-    adapter_grad = lax.psum(local_grads, ("fsdp", "dp"))
+    adapter_grad = jnp.sum(lax.all_gather(local_grads, ("fsdp", "dp")), axis=0)
     tokens_total = row_count * lax.axis_size("fsdp") * lax.axis_size("dp")
     step_rate = 0.01 / jnp.sqrt(jnp.float32(tokens_total))
     new_momentum = 0.9 * momentum + adapter_grad

time: 696 us -> 620 us (0.89)
  waiting for transfers between devices: 169 us -> 93.2 us
    psum x1 -> x0, waiting for transfers between devices: 83.1 us -> none  [per_device(): adapter_grad = lax.psum(local_grads, ('fsdp', 'dp'))]
    all_gather x0 -> x1, waiting for transfers between devices: none -> 7.18 us  [per_device(): adapter_grad = jnp.sum(lax.all_gather(local_grads, ('fsdp', 'dp')), axis=0)]
    unnamed x99 -> x100, local copies, waits for them, and re-layouts: 30.4 us -> 27.7 us
  transfers between devices with their start and end apart: 5 -> 5, of which waited for: 3 -> 3; matrix products, arithmetic and copies ran while one was open for 29% -> 34% of each run, Pallas kernels for 0% -> 0%
where the time goes in v1:
time: 620 us; the launch traced here: 612 us
  matrix products  327 us (53%)
  other arithmetic  111 us (18%)
  waiting for transfers between devices  93.2 us (15%)
  local copies, waits for them, and re-layouts  58.1 us (9%)
  between operations  14.7 us (2%)
  loops' own time  7.63 us (1%)
    dot_general x4, matrix products, block_scores(): jnp.einsum('qhe,khe->hqk', query_block, key_heads, preferred_element_type...  59.6 us
    convert_element_type x2, other arithmetic, one_block(): grad_scores = (probs * (grad_probs - inner)).astype(jnp.bfloat16)  55.6 us
    dot_general x7, matrix products, contract_trailing(): lax.dot_general(left, right, (((1,), (1,)), ((), ())), preferred_element_...  54.4 us
    dot_general x2, matrix products, one_block(): jnp.einsum('qhe,khe->hqk', grad_block, value_heads, preferred_element_typ...  51.9 us
    all_gather x1, waiting for transfers between devices, per_device(): lax.all_gather(w_qkv, 'fsdp', axis=0, tiled=True)  51.5 us
    dot_general x2, matrix products, one_block(): jnp.einsum('hqk,qhe->khe', probs.astype(jnp.bfloat16), grad_block, prefer...  36.3 us
    all_gather x1, waiting for transfers between devices, per_device(): lax.all_gather(w_proj, 'fsdp', axis=0, tiled=True)  31.9 us
    reduce_sum x2, other arithmetic, one_block(): totals = jnp.sum(raised, axis=-1, keepdims=True)  31.5 us
  transfers between devices with their start and end apart: 5, of which 3 were waited for; matrix products, arithmetic and copies ran while one was open for 34% of the time, Pallas kernels for 0%

profile of v1, /device:TPU:1, one launch (start us, length us, event | category | flops | bytes accessed | tf_op | source)
XLA Modules:
  0.0 611.6 jit_solution(1547512227022111034)
XLA Ops:
  23.1 51.5 %all-gather.7.cloned.1.call-done = bf16[1024,3072]{1,0:T(8,128)(2,1)} async-done(((bf16[64,3072]{1,0:T(8,128)(2,1)}), bf16[1024,3072]{1,0:T(8,128)(2,1)}) %all-gather.7.cloned.1.call-update) | async-done | bytes 6291472 | tf_op jit(solution)/shard_map/all_gather | solution.py:139
  74.7 9.0 %broadcast_add_fusion = f32[1024,3072]{1,0:T(8,128)S(1)} fusion(f32[3072]{0:T(1024)S(1)} %copy-done.51, bf16[1024,1024]{0,1:T(8,128)(2,1)S(1)} %copy-done.4, bf16[1024,3072]{1,0:T(8,128)(2,1)} %all-gather.7.cloned.1.call-done), kind=kOutput, calls=%fused_computation.68 | convolution fusion | flops 6445596672 | bytes 20983808 | tf_op jit(solution)/shard_map/dot_general | solution.py:157
  95.1 4.3 fusion.58
  104.8 100.5 %while.27 = (s32[]{:T(128)}, bf16[2,512,16,64]{1,3,2,0:T(8,128)(2,1)}, f32[2,16,512]{2,1,0:T(8,128)S(1)}, s32[2]{0:T(128)S(1)}, s32[1024]{0:T(1024)}, /*index=5*...) while((s32[]{:T(128)}, ...), condition=%wide.region_5.6_spmd, body=%wide.region_2.5_spmd.sunk | while | flops 2250236416 | bytes 134490384 | solution.py:71
  107.9 15.3 %fusion.152 = (f32[16,512]{1,0:T(8,128)S(1)}, f32[16,512,1024]{2,1,0:T(8,128)}) fusion(pred[512,1024]{1,0:T(8,128)(4,1)S(1)} %fusion.151, bf16[1024,16,64]{0,2,1:T(8,128)(2,1)S(1)} %get-tuple-element.403, bf16[1024,16,64]{0,2,1:T(8,128)(2,1)} %get-tuple-element.402, s32[]{:T(128)S(6)} %select_n.60), kind=kOutput, calls=%fused_computation.3.clone.1 | convolution fusion | flops 1098899456 | bytes 37257220 | tf_op jit(solution)/shard_map/while/body/eval_jaxpr/qhe,khe->hqk/dot_general | solution.py:46
  123.2 15.9 %fusion.153 = f32[16,512]{1,0:T(8,128)S(1)} fusion(f32[16,512,1024]{2,1,0:T(8,128)} %get-tuple-element.358, f32[16,512]{1,0:T(8,128)S(1)} %get-tuple-element.359, pred[512,1024]{1,0:T(8,128)(4,1)S(1)} %fusion.151), kind=kLoop, calls=%fused_computation.4.clone.1 | loop fusion | flops 33546240 | bytes 34144256 | tf_op jit(solution)/shard_map/while/body/eval_jaxpr/reduce_sum | solution.py:61
  139.1 14.7 %fusion.154 = bf16[2,512,16,64]{1,3,2,0:T(8,128)(2,1)S(1)} fusion(bf16[2,512,16,64]{1,3,2,0:T(8,128)(2,1)S(1)} %copy-done.13, s32[]{:T(128)S(6)} %copy.70, bf16[1024,16,64]{0,2,1:T(8,128)(2,1)S(1)} %copy-done, f32[16,512,1024]{2,1,0:T(8,128)} %get-tuple-element.358, f32[16,512]{1,0:T(8,128)S(1)} %fusion.153, f32[16,512]{1,0:T(8,128)S(1)} %get-tuple-element.359, ...), kind=kOutput, calls=%fused_computation.11.clone.1 | convolution fusion | flops 1116209152 | bytes 37289988 | tf_op jit(solution)/shard_map/while/body/eval_jaxpr/hqk,khe->qhe/dot_general | solution.py:63
  157.7 15.4 %fusion.152 = (f32[16,512]{1,0:T(8,128)S(1)}, f32[16,512,1024]{2,1,0:T(8,128)}) fusion(pred[512,1024]{1,0:T(8,128)(4,1)S(1)} %fusion.151, bf16[1024,16,64]{0,2,1:T(8,128)(2,1)S(1)} %get-tuple-element.403, bf16[1024,16,64]{0,2,1:T(8,128)(2,1)} %get-tuple-element.402, s32[]{:T(128)S(6)} %select_n.60), kind=kOutput, calls=%fused_computation.3.clone.1 | convolution fusion | flops 1098899456 | bytes 37257220 | tf_op jit(solution)/shard_map/while/body/eval_jaxpr/qhe,khe->hqk/dot_general | solution.py:46
  173.2 15.7 %fusion.153 = f32[16,512]{1,0:T(8,128)S(1)} fusion(f32[16,512,1024]{2,1,0:T(8,128)} %get-tuple-element.358, f32[16,512]{1,0:T(8,128)S(1)} %get-tuple-element.359, pred[512,1024]{1,0:T(8,128)(4,1)S(1)} %fusion.151), kind=kLoop, calls=%fused_computation.4.clone.1 | loop fusion | flops 33546240 | bytes 34144256 | tf_op jit(solution)/shard_map/while/body/eval_jaxpr/reduce_sum | solution.py:61
  188.9 14.9 %fusion.154 = bf16[2,512,16,64]{1,3,2,0:T(8,128)(2,1)S(1)} fusion(bf16[2,512,16,64]{1,3,2,0:T(8,128)(2,1)S(1)} %copy-done.13, s32[]{:T(128)S(6)} %copy.70, bf16[1024,16,64]{0,2,1:T(8,128)(2,1)S(1)} %copy-done, f32[16,512,1024]{2,1,0:T(8,128)} %get-tuple-element.358, f32[16,512]{1,0:T(8,128)S(1)} %fusion.153, f32[16,512]{1,0:T(8,128)S(1)} %get-tuple-element.359, ...), kind=kOutput, calls=%fused_computation.11.clone.1 | convolution fusion | flops 1116209152 | bytes 37289988 | tf_op jit(solution)/shard_map/while/body/eval_jaxpr/hqk,khe->qhe/dot_general | solution.py:63
  210.9 5.7 fusion.94
  219.2 16.9 %fusion.63 = f32[1024,4096]{1,0:T(8,128)} fusion(bf16[1024,4096]{1,0:T(8,128)(2,1)} %all-gather.11.cloned.1.call-done, f32[1024,1024]{0,1:T(8,128)} %copy-done.8, f32[1024]{0:T(1024)S(1)} %bitcast.157, f32[1024]{0:T(1024)S(1)} %bitcast.152, f32[1024]{0:T(1024)S(1)} %fusion.79, f32[1024]{0:T(1024)S(1)} %broadcast_multiply_fusion), kind=kOutput, calls=%fused_computation.96 | convolution fusion | flops 8595177472 | bytes 29376512 | tf_op jit(solution)/shard_map/dot_general | solution.py:184
  236.1 31.9 %all-gather.13.cloned.1.call-done = bf16[4096,1024]{1,0:T(8,128)(2,1)} async-done(((bf16[256,1024]{1,0:T(8,128)(2,1)}), bf16[4096,1024]{1,0:T(8,128)(2,1)}) %all-gather.13.cloned.1.call-update) | async-done | bytes 8388624 | tf_op jit(solution)/shard_map/all_gather | solution.py:144
  268.0 33.7 %multiply_reduce_fusion.1 = (f32[1024]{0:T(1024)S(1)}, f32[1024,1024]{0,1:T(8,128)}) fusion(f32[1024,1024]{0,1:T(8,128)} %copy-done.8, f32[1024]{0:T(1024)S(1)} %bitcast.153, f32[1024]{0:T(1024)S(1)} %broadcast_multiply_fusion, bf16[1024,4096]{1,0:T(8,128)(2,1)} %all-gather.11.cloned.1.call-done, f32[1024,4096]{1,0:T(8,128)} %fusion.63, ...), kind=kOutput, calls=%fused_computation.90 | convolution fusion | flops 17288921088 | bytes 44068864 | tf_op jit(solution)/shard_map/dot_general | solution.py:13
  301.7 4.7 fusion.90
  311.7 225.1 %while.28 = (s32[]{:T(128)}, f32[1024,16,64]{0,2,1:T(8,128)}, f32[1024,16,64]{0,2,1:T(8,128)}, bf16[2,512,16,64]{1,3,2,0:T(8,128)(2,1)}, s32[2]{0:T(128)S(1)}, /...) while((s32[]{:T(128)}, f32[1024,16,64]{0,2,1:T(8,128)}, ...), condition=%wide.region_12.13_spmd.clone, body=%wide.region_10.12_spmd.clone.sunk | while | flops 5502394880 | bytes 282831200 | solution.py:109
  313.4 14.4 %fusion.164 = f32[16,512,1024]{2,1,0:T(8,128)} fusion(bf16[1024,16,64]{0,2,1:T(8,128)(2,1)S(1)} %get-tuple-element.448, bf16[1024,16,64]{0,2,1:T(8,128)(2,1)} %get-tuple-element.446, s32[]{:T(128)S(6)} %select_n.64), kind=kOutput, calls=%fused_computation.37.clone.1 | convolution fusion | flops 1073741824 | bytes 36700164 | tf_op jit(solution)/shard_map/while/body/eval_jaxpr/qhe,khe->hqk/dot_general | solution.py:46
  331.1 26.0 %multiply_reduce_fusion.4 = (f32[16,512]{1,0:T(8,128)S(1)}, f32[16,512,1024]{2,1,0:T(8,128)}) fusion(f32[16,512,1024]{2,1,0:T(8,128)} %fusion.164, f32[16,512]{1,0:T(8,128)S(1)} %dynamic-slice_bitcast_fusion.2, pred[512,1024]{1,0:T(8,128)(4,1)S(1)} %fusion.165, bf16[1024,16,64]{0,2,1:T(8,128)(2,1)} %get-tuple-element.451, ...), kind=kOutput, calls=%fused_computation.20.clone.1 | convolution fusion | flops 1115676672 | bytes 70844416 | tf_op jit(solution)/shard_map/while/body/eval_jaxpr/qhe,khe->hqk/dot_general | solution.py:84
  357.0 27.8 %multiply_convert_fusion.7 = bf16[16,512,1024]{2,1,0:T(8,128)(2,1)} fusion(f32[16,512,1024]{2,1,0:T(8,128)} %get-tuple-element.371, f32[16,512,1024]{2,1,0:T(8,128)} %fusion.164, f32[16,512]{1,0:T(8,128)S(1)} %get-tuple-element.372, f32[16,512]{1,0:T(8,128)S(1)} %dynamic-slice_bitcast_fusion.2, pred[512,1024]{1,0:T(8,128)(4,1)S(1)} %fusion.165), kind=kLoop, calls=%fused_computation.19.clone.1 | loop fusion | flops 50331648 | bytes 84475904 | tf_op jit(solution)/shard_map/while/body/eval_jaxpr/convert_element_type | solution.py:94
  384.8 11.1 %bitcast_add_fusion.4 = f32[1024,16,64]{0,2,1:T(8,128)} fusion(f32[1024,16,64]{0,2,1:T(8,128)} %get-tuple-element.426, bf16[16,512,1024]{2,1,0:T(8,128)(2,1)} %multiply_convert_fusion.7, pred[]{:T(512)S(6)} %compare.3, bf16[1024,16,64]{0,2,1:T(8,128)(2,1)} %get-tuple-element.446, s32[]{:T(128)S(6)} %select_n.64), kind=kOutput, calls=%fused_computation.26.clone.1 | convolution fusion | flops 1076887552 | bytes 26214404 | tf_op jit(solution)/shard_map/while/body/eval_jaxpr/hqk,qhe->khe/dot_general | solution.py:101
  395.9 17.5 %bitcast_add_fusion.5 = f32[1024,16,64]{0,2,1:T(8,128)} fusion(f32[1024,16,64]{0,2,1:T(8,128)} %get-tuple-element.427, f32[16,512,1024]{2,1,0:T(8,128)} %fusion.164, f32[16,512]{1,0:T(8,128)S(1)} %dynamic-slice_bitcast_fusion.2, pred[512,1024]{1,0:T(8,128)(4,1)S(1)} %fusion.165, pred[]{:T(512)S(6)} %compare.3, ...), kind=kOutput, calls=%fused_computation.25.clone.1 | convolution fusion | flops 1109393408 | bytes 43548676 | tf_op jit(solution)/shard_map/while/body/eval_jaxpr/hqk,qhe->khe/dot_general | solution.py:87
  413.5 9.8 %fusion.166 = bf16[2,512,16,64]{1,3,2,0:T(8,128)(2,1)} fusion(bf16[2,512,16,64]{1,3,2,0:T(8,128)(2,1)} %get-tuple-element.428, s32[]{:T(128)S(6)} %copy.80, bf16[16,512,1024]{2,1,0:T(8,128)(2,1)} %multiply_convert_fusion.7, bf16[1024,16,64]{0,2,1:T(8,128)(2,1)S(1)} %get-tuple-element.448), kind=kOutput, calls=%fused_computation.32.clone.1 | convolution fusion | flops 1074790400 | bytes 19922948 | tf_op jit(solution)/shard_map/while/body/eval_jaxpr/hqk,khe->qhe/dot_general | solution.py:96
  424.5 14.4 %fusion.164 = f32[16,512,1024]{2,1,0:T(8,128)} fusion(bf16[1024,16,64]{0,2,1:T(8,128)(2,1)S(1)} %get-tuple-element.448, bf16[1024,16,64]{0,2,1:T(8,128)(2,1)} %get-tuple-element.446, s32[]{:T(128)S(6)} %select_n.64), kind=kOutput, calls=%fused_computation.37.clone.1 | convolution fusion | flops 1073741824 | bytes 36700164 | tf_op jit(solution)/shard_map/while/body/eval_jaxpr/qhe,khe->hqk/dot_general | solution.py:46
  442.2 26.0 %multiply_reduce_fusion.4 = (f32[16,512]{1,0:T(8,128)S(1)}, f32[16,512,1024]{2,1,0:T(8,128)}) fusion(f32[16,512,1024]{2,1,0:T(8,128)} %fusion.164, f32[16,512]{1,0:T(8,128)S(1)} %dynamic-slice_bitcast_fusion.2, pred[512,1024]{1,0:T(8,128)(4,1)S(1)} %fusion.165, bf16[1024,16,64]{0,2,1:T(8,128)(2,1)} %get-tuple-element.451, ...), kind=kOutput, calls=%fused_computation.20.clone.1 | convolution fusion | flops 1115676672 | bytes 70844416 | tf_op jit(solution)/shard_map/while/body/eval_jaxpr/qhe,khe->hqk/dot_general | solution.py:84
  468.1 27.8 %multiply_convert_fusion.7 = bf16[16,512,1024]{2,1,0:T(8,128)(2,1)} fusion(f32[16,512,1024]{2,1,0:T(8,128)} %get-tuple-element.371, f32[16,512,1024]{2,1,0:T(8,128)} %fusion.164, f32[16,512]{1,0:T(8,128)S(1)} %get-tuple-element.372, f32[16,512]{1,0:T(8,128)S(1)} %dynamic-slice_bitcast_fusion.2, pred[512,1024]{1,0:T(8,128)(4,1)S(1)} %fusion.165), kind=kLoop, calls=%fused_computation.19.clone.1 | loop fusion | flops 50331648 | bytes 84475904 | tf_op jit(solution)/shard_map/while/body/eval_jaxpr/convert_element_type | solution.py:94
  495.9 12.3 %bitcast_add_fusion.4 = f32[1024,16,64]{0,2,1:T(8,128)} fusion(f32[1024,16,64]{0,2,1:T(8,128)} %get-tuple-element.426, bf16[16,512,1024]{2,1,0:T(8,128)(2,1)} %multiply_convert_fusion.7, pred[]{:T(512)S(6)} %compare.3, bf16[1024,16,64]{0,2,1:T(8,128)(2,1)} %get-tuple-element.446, s32[]{:T(128)S(6)} %select_n.64), kind=kOutput, calls=%fused_computation.26.clone.1 | convolution fusion | flops 1076887552 | bytes 26214404 | tf_op jit(solution)/shard_map/while/body/eval_jaxpr/hqk,qhe->khe/dot_general | solution.py:101
  508.2 18.7 %bitcast_add_fusion.5 = f32[1024,16,64]{0,2,1:T(8,128)} fusion(f32[1024,16,64]{0,2,1:T(8,128)} %get-tuple-element.427, f32[16,512,1024]{2,1,0:T(8,128)} %fusion.164, f32[16,512]{1,0:T(8,128)S(1)} %dynamic-slice_bitcast_fusion.2, pred[512,1024]{1,0:T(8,128)(4,1)S(1)} %fusion.165, pred[]{:T(512)S(6)} %compare.3, ...), kind=kOutput, calls=%fused_computation.25.clone.1 | convolution fusion | flops 1109393408 | bytes 43548676 | tf_op jit(solution)/shard_map/while/body/eval_jaxpr/hqk,qhe->khe/dot_general | solution.py:87
  526.9 9.8 %fusion.166 = bf16[2,512,16,64]{1,3,2,0:T(8,128)(2,1)} fusion(bf16[2,512,16,64]{1,3,2,0:T(8,128)(2,1)} %get-tuple-element.428, s32[]{:T(128)S(6)} %copy.80, bf16[16,512,1024]{2,1,0:T(8,128)(2,1)} %multiply_convert_fusion.7, bf16[1024,16,64]{0,2,1:T(8,128)(2,1)S(1)} %get-tuple-element.448), kind=kOutput, calls=%fused_computation.32.clone.1 | convolution fusion | flops 1074790400 | bytes 19922948 | tf_op jit(solution)/shard_map/while/body/eval_jaxpr/hqk,khe->qhe/dot_general | solution.py:96
  546.5 17.0 %add_convert_fusion = bf16[1024,1024]{0,1:T(8,128)(2,1)} fusion(f32[1024,1024]{0,1:T(8,128)} %copy-done.8, f32[1024]{0:T(1024)S(1)} %bitcast.156, bf16[4096,1024]{1,0:T(8,128)(2,1)} %all-gather.13.cloned.1.call-done, f32[1024,4096]{1,0:T(8,128)} %fusion.63, f32[4096]{0:T(1024)S(1)} %copy-done.50), kind=kOutput, calls=%fused_computation.91 | convolution fusion | flops 8635023360 | bytes 31477760 | tf_op jit(solution)/shard_map/dot_general | solution.py:188
  571.1 9.6 %fusion.42 = f32[1024,1024]{0,1:T(8,128)S(1)} fusion(bf16[1024,3072]{1,0:T(8,128)(2,1)} %all-gather.7.cloned.1.call-done, bf16[1024,1024]{0,1:T(8,128)(2,1)S(1)} %bitcast.140, bf16[1024,1024]{0,1:T(8,128)(2,1)S(1)} %bitcast.147, bf16[1024,1024]{0,1:T(8,128)(2,1)S(1)} %bitcast.143), kind=kOutput, calls=%fused_computation.60 | convolution fusion | flops 6461325312 | bytes 16777216 | tf_op jit(solution)/shard_map/dot_general | solution.py:13
  588.8 5.4 copy.58
  594.2 7.2 %all-gather.15.cloned.1.call-done = f32[128,1024,4]{1,2,0:T(4,128)} async-done(((f32[4,1024,4]{1,2,0:T(4,128)}), f32[128,1024,4]{1,2,0:T(4,128)}) %all-gather.15.cloned.1.call-update) | async-done | bytes 2097168 | tf_op jit(solution)/shard_map/all_gather | solution.py:236
  (200 shorter events, 85.2 us)
Async XLA Ops:
  7.2 5.8 copy-start.42
  7.2 6.4 %copy-start.43 = (f32[2,1024]{1,0:T(2,128)S(1)}, f32[2,1024]{1,0:T(2,128)}, u32[]{:S(2)}) copy-start(f32[2,1024]{1,0:T(2,128)} %param.22) | copy-start | bytes 24580
  7.2 67.5 %all-gather.7.cloned.1.call-start = ((), (), s32[]{:S(2)}) async-start(), calls=%async_computation | async-start | bytes 6684672 | tf_op jit(solution)/shard_map/all_gather | solution.py:139
  7.9 203.0 %all-gather.9.cloned.1.call-start = ((), (), s32[]{:S(2)}) async-start(), calls=%async_computation.1 | async-start | bytes 2228224 | tf_op jit(solution)/shard_map/all_gather | solution.py:140
  8.7 210.5 %all-gather.11.cloned.1.call-start = ((), (), s32[]{:S(2)}) async-start(), calls=%async_computation.2 | async-start | bytes 8912896 | tf_op jit(solution)/shard_map/all_gather | solution.py:143
  9.4 258.5 %all-gather.13.cloned.1.call-start = ((), (), s32[]{:S(2)}) async-start(), calls=%async_computation.3 | async-start | bytes 8912896 | tf_op jit(solution)/shard_map/all_gather | solution.py:144
  10.0 591.4 %all-gather.15.cloned.1.call-start = ((), (), s32[]{:S(2)}) async-start(), calls=%async_computation.4 | async-start | bytes 2162688 | tf_op jit(solution)/shard_map/all_gather | solution.py:236
  10.0 5.8 copy-start.23
  15.9 79.2 %copy-start.19 = (bf16[4,1024,4]{1,2,0:T(4,128)(2,1)}, bf16[4,1024,4]{1,2,0:T(4,128)(2,1)S(1)}, u32[]{:S(2)}) copy-start(bf16[4,1024,4]{1,2,0:T(4,128)(2,1)S(1)} %convert_element_type.81) | copy-start | bytes 98308
  16.7 58.0 %copy-start.51 = (f32[3072]{0:T(1024)S(1)}, f32[3072]{0:T(1024)}, u32[]{:S(2)}) copy-start(f32[3072]{0:T(1024)} %param.25) | copy-start | bytes 36868
  18.0 67.5 %copy-start.27 = (bf16[1024,4]{0,1:T(4,128)(2,1)}, bf16[1024,4]{0,1:T(4,128)(2,1)S(1)}, u32[]{:S(2)}) copy-start(bf16[1024,4]{0,1:T(4,128)(2,1)S(1)} %convolution_convert_fusion.1) | copy-start | bytes 24580
  18.4 76.6 %copy-start.29 = (bf16[1024,4]{0,1:T(4,128)(2,1)}, bf16[1024,4]{0,1:T(4,128)(2,1)S(1)}, u32[]{:S(2)}) copy-start(bf16[1024,4]{0,1:T(4,128)(2,1)S(1)} %convolution_convert_fusion) | copy-start | bytes 24580
  18.4 56.3 %copy-start.4 = (bf16[1024,1024]{0,1:T(8,128)(2,1)S(1)}, bf16[1024,1024]{0,1:T(8,128)(2,1)}, u32[]{:S(2)}) copy-start(bf16[1024,1024]{0,1:T(8,128)(2,1)} %copy-done.3) | copy-start | bytes 6291460
  83.7 5.2 copy-start.11
  123.2 15.9 %copy-start = (bf16[1024,16,64]{0,2,1:T(8,128)(2,1)S(1)}, bf16[1024,16,64]{0,2,1:T(8,128)(2,1)}, u32[]{:S(2)}) copy-start(bf16[1024,16,64]{0,2,1:T(8,128)(2,1)} %get-tuple-element.404) | copy-start | bytes 6291460 | tf_op jit(solution)/shard_map/while
  123.2 15.9 %copy-start.13 = (bf16[2,512,16,64]{1,3,2,0:T(8,128)(2,1)S(1)}, bf16[2,512,16,64]{1,3,2,0:T(8,128)(2,1)}, u32[]{:S(2)}) copy-start(bf16[2,512,16,64]{1,3,2,0:T(8,128)(2,1)} %get-tuple-element.386) | copy-start | bytes 6291460 | tf_op jit(solution)/shard_map/while
  173.1 15.7 %copy-start = (bf16[1024,16,64]{0,2,1:T(8,128)(2,1)S(1)}, bf16[1024,16,64]{0,2,1:T(8,128)(2,1)}, u32[]{:S(2)}) copy-start(bf16[1024,16,64]{0,2,1:T(8,128)(2,1)} %get-tuple-element.404) | copy-start | bytes 6291460 | tf_op jit(solution)/shard_map/while
  173.2 15.7 %copy-start.13 = (bf16[2,512,16,64]{1,3,2,0:T(8,128)(2,1)S(1)}, bf16[2,512,16,64]{1,3,2,0:T(8,128)(2,1)}, u32[]{:S(2)}) copy-start(bf16[2,512,16,64]{1,3,2,0:T(8,128)(2,1)} %get-tuple-element.386) | copy-start | bytes 6291460 | tf_op jit(solution)/shard_map/while
  205.2 5.7 copy-start.47
  219.2 48.8 %copy-start.49 = (f32[4096]{0:T(1024)S(1)}, f32[4096]{0:T(1024)}, u32[]{:S(2)}) copy-start(f32[4096]{0:T(1024)} %param.28) | copy-start | bytes 49156
  301.6 4.7 copy-start.15
  301.7 4.7 copy-start.48
  312.1 17.5 %copy-start.17 = (f32[2,16,512]{2,1,0:T(8,128)}, f32[2,16,512]{2,1,0:T(8,128)S(1)}, u32[]{:S(2)}) copy-start(f32[2,16,512]{2,1,0:T(8,128)S(1)} %get-tuple-element.449) | copy-start | bytes 196612 | tf_op jit(solution)/shard_map/while
  413.5 9.8 %copy-start.18 = (f32[2,16,512]{2,1,0:T(8,128)S(1)}, f32[2,16,512]{2,1,0:T(8,128)}, u32[]{:S(2)}) copy-start(f32[2,16,512]{2,1,0:T(8,128)} %copy-done.17) | copy-start | bytes 196612 | tf_op jit(solution)/shard_map/while
  423.2 17.5 %copy-start.17 = (f32[2,16,512]{2,1,0:T(8,128)}, f32[2,16,512]{2,1,0:T(8,128)S(1)}, u32[]{:S(2)}) copy-start(f32[2,16,512]{2,1,0:T(8,128)S(1)} %get-tuple-element.449) | copy-start | bytes 196612 | tf_op jit(solution)/shard_map/while
  526.9 9.8 %copy-start.18 = (f32[2,16,512]{2,1,0:T(8,128)S(1)}, f32[2,16,512]{2,1,0:T(8,128)}, u32[]{:S(2)}) copy-start(f32[2,16,512]{2,1,0:T(8,128)} %copy-done.17) | copy-start | bytes 196612 | tf_op jit(solution)/shard_map/while
  571.1 9.7 %copy-start.2 = (bf16[1024,1024]{0,1:T(8,128)(2,1)S(1)}, bf16[1024,1024]{0,1:T(8,128)(2,1)}, u32[]{:S(2)}) copy-start(bf16[1024,1024]{0,1:T(8,128)(2,1)} %copy-done.1) | copy-start | bytes 6291460
  571.1 9.7 %copy-start.26 = (f32[1024]{0:T(1024)S(1)}, f32[1024]{0:T(1024)}, u32[]{:S(2)}) copy-start(f32[1024]{0:T(1024)} %copy-done.25) | copy-start | bytes 12292
  571.1 9.7 %copy-start.38 = (f32[1,1024]{1,0:T(1,128)S(1)}, f32[1,1024]{1,0:T(1,128)}, u32[]{:S(2)}) copy-start(f32[1,1024]{1,0:T(1,128)} %copy-done.37) | copy-start | bytes 12292
  588.8 14.7 %copy-start.24 = (f32[4,1024,4]{1,2,0:T(4,128)S(1)}, f32[4,1024,4]{1,2,0:T(4,128)}, u32[]{:S(2)}) copy-start(f32[4,1024,4]{1,2,0:T(4,128)} %param.31) | copy-start | bytes 196612
  588.8 14.7 %copy-start.32 = (f32[4,1024,4]{1,2,0:T(4,128)S(1)}, f32[4,1024,4]{1,2,0:T(4,128)}, u32[]{:S(2)}) copy-start(f32[4,1024,4]{1,2,0:T(4,128)} %param.32) | copy-start | bytes 196612
  588.8 15.4 %copy-start.31 = (f32[4,1024,4]{1,2,0:T(4,128)S(1)}, f32[4,1024,4]{1,2,0:T(4,128)}, u32[]{:S(2)}) copy-start(f32[4,1024,4]{1,2,0:T(4,128)} %param.33) | copy-start | bytes 196612
  (30 other events, 69.1 us)
Sparse Core Ops, SparseCore 0:
  10.3 64.3 all-gather.6
  76.9 39.9 all-gather.8
  119.0 73.6 all-gather.10
  194.8 73.1 all-gather.12
  546.6 54.7 all-gather.14
